TPU v7x, 32 devices: a whole 2x2x4 slice. The times are simulated.
32 devices in a mesh: dp: 8 (over y, x, core), seq: 4 (over z).
Axes of the slice: x: 2, y: 2, z: 4, core: 2. Of those that a mesh axis runs over, the one named last changes fastest.
Arguments:
- inputs: bfloat16 [24, 1024, 768], P('dp', 'seq'), may hold values from -6 to 6
- cotangent: bfloat16 [24, 1024, 768], P('dp', 'seq'), may hold values from -6 to 6
- lengths: int32 [24], P('dp'), may hold values from 100 to 1024, as said below
- predicted: int32 [24, 1024], P('dp', 'seq'), may hold values from 0 to 69
- norm1_gain: float32 [768], replicated, may hold values from 0.1 to 1.9
- norm1_shift: float32 [768], replicated, may hold values from -4 to 4
- w_query: bfloat16 [768, 768], replicated, may hold values from -0.3125 to 0.3125
- b_query: float32 [768], replicated, may hold values from -6 to 6
- w_key: bfloat16 [768, 768], replicated, may hold values from -0.3125 to 0.3125
- b_key: float32 [768], replicated, may hold values from -6 to 6
- w_value: bfloat16 [768, 768], replicated, may hold values from -0.21875 to 0.21875
- b_value: float32 [768], replicated, may hold values from -6 to 6
- w_out: bfloat16 [768, 768], replicated, may hold values from -2 to 2
- b_out: float32 [768], replicated, may hold values from -6 to 6
- norm2_gain: float32 [768], replicated, may hold values from 0.1 to 1.9
- norm2_shift: float32 [768], replicated, may hold values from -4 to 4
- w_up: bfloat16 [768, 3072], replicated, may hold values from -0.21875 to 0.21875
- b_up: float32 [3072], replicated, may hold values from -6 to 6
- w_down: bfloat16 [3072, 768], replicated, may hold values from -0.109375 to 0.109375
- b_down: float32 [768], replicated, may hold values from -6 to 6
Outputs:
- result: bfloat16 [24, 1024, 768], P('dp', 'seq')
- grad_inputs: bfloat16 [24, 1024, 768], P('dp', 'seq')
- grad_norm1_gain: float32 [768], replicated
- grad_norm1_shift: float32 [768], replicated
- grad_w_query: float32 [768, 768], replicated
- grad_b_query: float32 [768], replicated
- grad_w_key: float32 [768, 768], replicated
- grad_b_key: float32 [768], replicated
- grad_w_value: float32 [768, 768], replicated
- grad_b_value: float32 [768], replicated
- grad_w_out: float32 [768, 768], replicated
- grad_b_out: float32 [768], replicated
- grad_norm2_gain: float32 [768], replicated
- grad_norm2_shift: float32 [768], replicated
- grad_w_up: float32 [768, 3072], replicated
- grad_b_up: float32 [3072], replicated
- grad_w_down: float32 [3072, 768], replicated
- grad_b_down: float32 [768], replicated
- histogram: int32 [70], replicated
Inputs may be any that keep to these rules, and one draw needn't show every extreme that they name: Some sequence has 1024 real codons and some has 100; the codons from position lengths[s] on are padding.
All inputs are finite; a program needn't handle non-finite values.
Results may differ from a plain program's by a relative error of at most 0.014.
The roundings to bfloat16 on the way count: a program that leaves them out, or rounds other values in their place, can miss the bound.
Values may be sent and summed in bfloat16 or wider, within the bound.
No kernel may reach another device: no remote copies, remote signals or barrier semaphores. Data moves between devices by JAX's collectives and lax.ppermute only.
A program may use at most 192 MiB of HBM per device.

v0:
```python
import jax
import jax.numpy as jnp
from jax import lax
from jax.sharding import PartitionSpec as P

HEAD = 64
CLASSES = 70
epsilon = 1e-05


def matmul(left, right):
    return jnp.dot(left, right, preferred_element_type=jnp.float32)


def matmul_left(left, right):
    return lax.dot_general(
        left, right, (((0,), (0,)), ((), ())), preferred_element_type=jnp.float32
    )


def matmul_right(left, right):
    return lax.dot_general(
        left, right, (((1,), (1,)), ((), ())), preferred_element_type=jnp.float32
    )


def layer_norm(value, gain, shift):
    centre = value - jnp.mean(value, axis=-1, keepdims=True)
    scale = lax.rsqrt(jnp.mean(centre * centre, axis=-1, keepdims=True) + epsilon)
    return centre * scale * gain + shift


def gelu(value):
    return jax.nn.gelu(value, approximate=False)


def rotate(value, direction):
    count = value.shape[-3]
    half = value.shape[-1] // 2
    frequency = 10000.0 ** (-jnp.arange(half, dtype=jnp.float32) / half)
    angle = jnp.arange(count, dtype=jnp.float32)[:, None] * frequency[None, :]
    cosine = jnp.cos(angle)[:, None, :]
    sine = direction * jnp.sin(angle)[:, None, :]
    first = value[..., :half]
    second = value[..., half:]
    return jnp.concatenate(
        [first * cosine - second * sine, second * cosine + first * sine], axis=-1
    )


def attend_forward(query, key, value, valid, block):
    count, heads, size = query.shape
    scale = HEAD ** (-0.5)
    blocks = query.reshape(count // block, block, heads, size)

    def visit(query_block):
        scores = (
            jnp.einsum("qhd,khd->hqk", query_block, key, preferred_element_type=jnp.float32) * scale
        )
        scores = jnp.where(valid[None, None, :], scores, -1e30)
        peak = jnp.max(scores, axis=-1, keepdims=True)
        total = jnp.sum(jnp.exp(scores - peak), axis=-1, keepdims=True)
        logsum = peak + jnp.log(total)
        weights = jnp.exp(scores - logsum).astype(jnp.bfloat16)
        mixed = jnp.einsum("hqk,khd->qhd", weights, value, preferred_element_type=jnp.float32)
        return (mixed.astype(jnp.bfloat16), logsum[..., 0])

    mixed, logsum = lax.map(visit, blocks)
    return (mixed.reshape(count, heads * size), logsum)


def attend_backward(query, key, value, valid, logsum, grad_mixed, block):
    count, heads, size = query.shape
    number = count // block
    scale = HEAD ** (-0.5)
    query_blocks = query.reshape(number, block, heads, size)
    grad_blocks = grad_mixed.reshape(number, block, heads, size)

    def visit(carry, item):
        grad_key, grad_value = carry
        query_block, grad_block, logsum_block = item
        scores = (
            jnp.einsum("qhd,khd->hqk", query_block, key, preferred_element_type=jnp.float32) * scale
        )
        scores = jnp.where(valid[None, None, :], scores, -1e30)
        weights = jnp.exp(scores - logsum_block[..., None])
        weights_low = weights.astype(jnp.bfloat16)
        grad_weights = jnp.einsum(
            "qhd,khd->hqk", grad_block, value, preferred_element_type=jnp.float32
        )
        inner = jnp.sum(weights * grad_weights, axis=-1, keepdims=True)
        grad_scores = (weights * (grad_weights - inner)).astype(jnp.bfloat16)
        grad_query = (
            jnp.einsum("hqk,khd->qhd", grad_scores, key, preferred_element_type=jnp.float32) * scale
        )
        grad_key = (
            grad_key
            + jnp.einsum(
                "hqk,qhd->khd", grad_scores, query_block, preferred_element_type=jnp.float32
            )
            * scale
        )
        grad_value = grad_value + jnp.einsum(
            "hqk,qhd->khd", weights_low, grad_block, preferred_element_type=jnp.float32
        )
        return ((grad_key, grad_value), grad_query)

    start = jnp.zeros((count, heads, size), jnp.float32)
    (grad_key, grad_value), grad_query = lax.scan(
        visit, (start, start), (query_blocks, grad_blocks, logsum)
    )
    grad_query = rotate(grad_query.reshape(count, heads, size), -1.0).astype(jnp.bfloat16)
    grad_key = rotate(grad_key, -1.0).astype(jnp.bfloat16)
    grad_value = grad_value.astype(jnp.bfloat16)
    return (
        grad_query.reshape(count, heads * size),
        grad_key.reshape(count, heads * size),
        grad_value.reshape(count, heads * size),
    )


def on_device(
    inputs,
    cotangent,
    lengths,
    predicted,
    norm1_gain,
    norm1_shift,
    w_query,
    b_query,
    w_key,
    b_key,
    w_value,
    b_value,
    w_out,
    b_out,
    norm2_gain,
    norm2_shift,
    w_up,
    b_up,
    w_down,
    b_down,
):
    seqs, span, width = inputs.shape
    tokens = seqs * span
    hidden_width = w_up.shape[1]
    flat_in = inputs.reshape(tokens, width).astype(jnp.float32)
    normed_full, norm1_back = jax.vjp(layer_norm, flat_in, norm1_gain, norm1_shift)
    normed = normed_full.astype(jnp.bfloat16)
    query = (matmul(normed, w_query) + b_query).astype(jnp.bfloat16).reshape(seqs, span, width)
    key = (matmul(normed, w_key) + b_key).astype(jnp.bfloat16).reshape(seqs, span, width)
    value = (matmul(normed, w_value) + b_value).astype(jnp.bfloat16).reshape(seqs, span, width)
    head_query, head_key, head_value = (
        lax.all_to_all(query, "seq", split_axis=2, concat_axis=1, tiled=True),
        lax.all_to_all(key, "seq", split_axis=2, concat_axis=1, tiled=True),
        lax.all_to_all(value, "seq", split_axis=2, concat_axis=1, tiled=True),
    )
    count = head_query.shape[1]
    heads = head_query.shape[2] // HEAD
    shaped = (seqs, count, heads, HEAD)
    rot_query = rotate(head_query.reshape(shaped).astype(jnp.float32), 1.0).astype(jnp.bfloat16)
    rot_key = rotate(head_key.reshape(shaped).astype(jnp.float32), 1.0).astype(jnp.bfloat16)
    head_value = head_value.reshape(shaped)
    valid = jnp.arange(count)[None, :] < lengths[:, None]
    block = min(count, 512)
    mixed, logsum = lax.map(
        lambda item: attend_forward(item[0], item[1], item[2], item[3], block),
        (rot_query, rot_key, head_value, valid),
    )
    attended = lax.all_to_all(mixed, "seq", split_axis=1, concat_axis=2, tiled=True).reshape(
        tokens, width
    )
    middle = flat_in + matmul(attended, w_out) + b_out
    normed2_full, norm2_back = jax.vjp(layer_norm, middle, norm2_gain, norm2_shift)
    normed2 = normed2_full.astype(jnp.bfloat16)
    hidden_in = matmul(normed2, w_up) + b_up
    hidden = gelu(hidden_in).astype(jnp.bfloat16)
    result = (
        (middle + matmul(hidden, w_down) + b_down).astype(jnp.bfloat16).reshape(seqs, span, width)
    )
    grad_result = cotangent.reshape(tokens, width)
    grad_result_full = grad_result.astype(jnp.float32)
    grad_w_down = matmul_left(hidden, grad_result)
    grad_b_down = jnp.sum(grad_result_full, axis=0)
    unused, gelu_back = jax.vjp(gelu, hidden_in)
    grad_hidden_in = gelu_back(matmul_right(grad_result, w_down))[0].astype(jnp.bfloat16)
    grad_w_up = matmul_left(normed2, grad_hidden_in)
    grad_b_up = jnp.sum(grad_hidden_in.astype(jnp.float32), axis=0)
    grad_from_norm2, grad_norm2_gain, grad_norm2_shift = norm2_back(
        matmul_right(grad_hidden_in, w_up)
    )
    grad_middle = grad_result_full + grad_from_norm2
    grad_branch = grad_middle.astype(jnp.bfloat16)
    grad_w_out = matmul_left(attended, grad_branch)
    grad_b_out = jnp.sum(grad_middle, axis=0)
    grad_attended = matmul_right(grad_branch, w_out).astype(jnp.bfloat16).reshape(seqs, span, width)
    grad_mixed = lax.all_to_all(
        grad_attended, "seq", split_axis=2, concat_axis=1, tiled=True
    ).reshape(shaped)
    grad_query, grad_key, grad_value = lax.map(
        lambda item: attend_backward(item[0], item[1], item[2], item[3], item[4], item[5], block),
        (rot_query, rot_key, head_value, valid, logsum, grad_mixed),
    )
    back_query, back_key, back_value = (
        lax.all_to_all(grad_query, "seq", split_axis=1, concat_axis=2, tiled=True),
        lax.all_to_all(grad_key, "seq", split_axis=1, concat_axis=2, tiled=True),
        lax.all_to_all(grad_value, "seq", split_axis=1, concat_axis=2, tiled=True),
    )
    back_query = back_query.reshape(tokens, width)
    back_key = back_key.reshape(tokens, width)
    back_value = back_value.reshape(tokens, width)
    grad_w_query = matmul_left(normed, back_query)
    grad_w_key = matmul_left(normed, back_key)
    grad_w_value = matmul_left(normed, back_value)
    grad_b_query = jnp.sum(back_query.astype(jnp.float32), axis=0)
    grad_b_key = jnp.sum(back_key.astype(jnp.float32), axis=0)
    grad_b_value = jnp.sum(back_value.astype(jnp.float32), axis=0)
    grad_normed = (
        matmul_right(back_query, w_query)
        + matmul_right(back_key, w_key)
        + matmul_right(back_value, w_value)
    )
    grad_from_norm1, grad_norm1_gain, grad_norm1_shift = norm1_back(grad_normed)
    grad_inputs = (grad_middle + grad_from_norm1).astype(jnp.bfloat16).reshape(seqs, span, width)
    position = lax.axis_index("seq") * span + jnp.arange(span)
    live = position[None, :] < lengths[:, None]
    classes = jnp.arange(CLASSES)
    counts = jnp.sum(
        jnp.where(live[:, :, None] & (predicted[:, :, None] == classes), 1.0, 0.0), axis=(0, 1)
    )
    (
        grad_norm1_gain,
        grad_norm1_shift,
        grad_b_query,
        grad_b_key,
        grad_b_value,
        grad_b_out,
        grad_norm2_gain,
        grad_norm2_shift,
        grad_b_up,
        grad_b_down,
        counts,
    ) = lax.psum(
        (
            grad_norm1_gain,
            grad_norm1_shift,
            grad_b_query,
            grad_b_key,
            grad_b_value,
            grad_b_out,
            grad_norm2_gain,
            grad_norm2_shift,
            grad_b_up,
            grad_b_down,
            counts,
        ),
        ("dp", "seq"),
    )
    part_query = grad_w_query.reshape(-1)
    part_key = grad_w_key.reshape(-1)
    part_value = grad_w_value.reshape(-1)
    part_out = grad_w_out.reshape(-1)
    part_up = grad_w_up.reshape(-1)
    part_down = grad_w_down.reshape(-1)
    part_query, part_key, part_value, part_out, part_up, part_down = (
        lax.psum_scatter(part_query, ("dp", "seq"), scatter_dimension=0, tiled=True),
        lax.psum_scatter(part_key, ("dp", "seq"), scatter_dimension=0, tiled=True),
        lax.psum_scatter(part_value, ("dp", "seq"), scatter_dimension=0, tiled=True),
        lax.psum_scatter(part_out, ("dp", "seq"), scatter_dimension=0, tiled=True),
        lax.psum_scatter(part_up, ("dp", "seq"), scatter_dimension=0, tiled=True),
        lax.psum_scatter(part_down, ("dp", "seq"), scatter_dimension=0, tiled=True),
    )
    part_query, part_key, part_value, part_out, part_up, part_down = (
        lax.all_gather(part_query, ("dp", "seq"), axis=0, tiled=True),
        lax.all_gather(part_key, ("dp", "seq"), axis=0, tiled=True),
        lax.all_gather(part_value, ("dp", "seq"), axis=0, tiled=True),
        lax.all_gather(part_out, ("dp", "seq"), axis=0, tiled=True),
        lax.all_gather(part_up, ("dp", "seq"), axis=0, tiled=True),
        lax.all_gather(part_down, ("dp", "seq"), axis=0, tiled=True),
    )
    return (
        result,
        grad_inputs,
        grad_norm1_gain,
        grad_norm1_shift,
        part_query.reshape(width, width),
        grad_b_query,
        part_key.reshape(width, width),
        grad_b_key,
        part_value.reshape(width, width),
        grad_b_value,
        part_out.reshape(width, width),
        grad_b_out,
        grad_norm2_gain,
        grad_norm2_shift,
        part_up.reshape(width, hidden_width),
        grad_b_up,
        part_down.reshape(hidden_width, width),
        grad_b_down,
        counts.astype(jnp.int32),
    )


def solution(mesh):
    return jax.shard_map(
        on_device,
        mesh=mesh,
        in_specs=(
            P("dp", "seq", None),
            P("dp", "seq", None),
            P("dp"),
            P("dp", "seq"),
            P(),
            P(),
            P(),
            P(),
            P(),
            P(),
            P(),
            P(),
            P(),
            P(),
            P(),
            P(),
            P(),
            P(),
            P(),
            P(),
        ),
        out_specs=(
            P("dp", "seq", None),
            P("dp", "seq", None),
            P(),
            P(),
            P(),
            P(),
            P(),
            P(),
            P(),
            P(),
            P(),
            P(),
            P(),
            P(),
            P(),
            P(),
            P(),
            P(),
            P(),
        ),
        check_vma=False,
    )
```

profile of v0, /device:TPU:0, one launch (start us, length us, event | category | flops | bytes accessed | tf_op | source)
XLA Modules:
  0.0 1592.5 jit_solution(14903146880478550544)
XLA Ops:
  15.9 6.3 all-to-all-start.1
  22.2 3.7 add_convert_fusion.8
  26.0 3.6 copy.108
  29.5 29.6 %all-to-all-done.1 = bf16[3,256,768]{1,0,2:T(4,128)(2,1)S(1)} async-done(((bf16[3,256,768]{1,0,2:T(4,128)(2,1)}), bf16[3,256,768]{1,0,2:T(4,128)(2,1)S(1)}, u32[]{:S(2)}, u32[]{:S(2)}) %all-to-all-start.1) | async-done | bytes 1179680 | tf_op jit(solution)/shard_map/all_to_all | solution.py:155
  59.2 4.4 all-to-all-start
  70.5 29.5 %all-to-all-done = bf16[3,256,768]{1,0,2:T(4,128)(2,1)} async-done(((bf16[3,256,768]{1,0,2:T(4,128)(2,1)}), bf16[3,256,768]{1,0,2:T(4,128)(2,1)}, u32[]{:S(2)}, u32[]{:S(2)}) %all-to-all-start) | async-done | bytes 1179680 | tf_op jit(solution)/shard_map/all_to_all | solution.py:154
  100.1 4.8 all-to-all-start.2
  116.0 25.4 %all-to-all-done.2 = bf16[3,256,768]{1,0,2:T(4,128)(2,1)} async-done(((bf16[3,256,768]{1,0,2:T(4,128)(2,1)}), bf16[3,256,768]{1,0,2:T(4,128)(2,1)}, u32[]{:S(2)}, u32[]{:S(2)}) %all-to-all-start.2) | async-done | bytes 1179680 | tf_op jit(solution)/shard_map/all_to_all | solution.py:156
  153.6 43.8 %while.54 = (s32[]{:T(128)}, bf16[3,1024,192]{1,2,0:T(8,128)(2,1)}, f32[3,2,3,512]{3,2,1,0:T(4,128)}, bf16[3,1024,3,64]{1,3,2,0:T(8,128)(2,1)}, bf16[3,1024,3,64...) while((s32[]{:T(128)}, bf16[3,1024,192]{1,2,0:T(8,128)(2,1)}, ...), condition=%wide.region_7.8_spmd, body=%wide.region_2.7_spmd.sunk | while | flops 420051456 | bytes 28114308 | solution.py:166
  156.9 8.6 while.57
  171.5 8.6 while.57
  186.0 8.6 while.57
  197.4 4.3 copy.117
  201.6 51.3 %all_to_all.108 = bf16[3,1024,192]{2,0,1:T(4,128)(2,1)S(1)} all-to-all(bf16[3,1024,192]{2,0,1:T(4,128)(2,1)} %copy.117), channel_id=1, replica_groups=mesh['dp'=8,'seq'=4] {'seq'}, dimensions={1} | all-to-all | bytes 2359296 | tf_op jit(solution)/shard_map/all_to_all | solution.py:170
  262.4 7.1 fusion.73
  269.6 27.3 %convert_reduce_fusion = (f32[3072]{0:T(1024)}, bf16[768,3072]{1,0:T(8,128)(2,1)S(1)}, f32[768,3072]{1,0:T(8,128)}) fusion(f32[768,3072]{1,0:T(8,128)S(1)} %fusion.73, f32[3072]{0:T(1024)S(1)} %copy-done.58, bf16[768,768]{1,0:T(8,128)(2,1)S(1)} %bitcast.247, bf16[3072,768]{1,0:T(8,128)(2,1)S(1)} %bitcast.262), kind=kOutput, calls=%fused_computation.74 | convolution fusion | flops 3800822784 | bytes 29515776 | tf_op jit(solution)/shard_map/dot_general | solution.py:22
  296.9 4.8 multiply_reduce_fusion.1
  307.3 4.0 all-to-all-start.4
  311.3 36.0 %all-to-all-done.4 = bf16[3,256,768]{1,0,2:T(4,128)(2,1)S(1)} async-done(((bf16[3,256,768]{1,0,2:T(4,128)(2,1)}), bf16[3,256,768]{1,0,2:T(4,128)(2,1)S(1)}, u32[]{:S(2)}, u32[]{:S(2)}) %all-to-all-start.4) | async-done | bytes 1179680 | tf_op jit(solution)/shard_map/all_to_all | solution.py:197
  352.8 180.7 %while.56 = (s32[]{:T(128)}, bf16[3,1024,192]{1,2,0:T(8,128)(2,1)}, bf16[3,1024,192]{1,2,0:T(8,128)(2,1)}, bf16[3,1024,192]{1,2,0:T(8,128)(2,1)}, bf16[3,1024,3,...) while((s32[]{:T(128)}, bf16[3,1024,192]{1,2,0:T(8,128)(2,1)}, ...), condition=%wide.region_16.17_spmd, body=%wide.region_12.16_spmd.sunk | while | flops 1034713664 | bytes 145711024 | solution.py:200
  359.7 48.1 %while.58 = (s32[]{:T(128)}, f32[1024,3,64]{0,2,1:T(8,128)S(1)}, f32[1024,3,64]{0,2,1:T(8,128)}, f32[2,512,3,64]{1,0,3,2:T(2,128)}, bf16[2,512,3,64]{1,3,2,0:T(8...) while((s32[]{:T(128)}, f32[1024,3,64]{0,2,1:T(8,128)S(1)}, ...), condition=%wide.region_15.15_spmd.clone, body=%wide.region_13.14_spmd.clone.sunk | while | flops 1031305728 | bytes 117228824 | solution.py:109
  375.6 8.0 dynamic_update_slice.50
  394.5 3.8 fusion.154
  399.8 8.0 dynamic_update_slice.50
  420.0 48.1 %while.58 = (s32[]{:T(128)}, f32[1024,3,64]{0,2,1:T(8,128)S(1)}, f32[1024,3,64]{0,2,1:T(8,128)}, f32[2,512,3,64]{1,0,3,2:T(2,128)}, bf16[2,512,3,64]{1,3,2,0:T(8...) while((s32[]{:T(128)}, f32[1024,3,64]{0,2,1:T(8,128)S(1)}, ...), condition=%wide.region_15.15_spmd.clone, body=%wide.region_13.14_spmd.clone.sunk | while | flops 1031305728 | bytes 117228824 | solution.py:109
  435.8 8.0 dynamic_update_slice.50
  454.8 3.8 fusion.154
  460.0 8.0 dynamic_update_slice.50
  480.2 48.1 %while.58 = (s32[]{:T(128)}, f32[1024,3,64]{0,2,1:T(8,128)S(1)}, f32[1024,3,64]{0,2,1:T(8,128)}, f32[2,512,3,64]{1,0,3,2:T(2,128)}, bf16[2,512,3,64]{1,3,2,0:T(8...) while((s32[]{:T(128)}, f32[1024,3,64]{0,2,1:T(8,128)S(1)}, ...), condition=%wide.region_15.15_spmd.clone, body=%wide.region_13.14_spmd.clone.sunk | while | flops 1031305728 | bytes 117228824 | solution.py:109
  496.1 8.0 dynamic_update_slice.50
  515.0 3.8 fusion.154
  520.3 8.0 dynamic_update_slice.50
  533.4 4.0 copy.126
  537.5 4.6 all-to-all-start.7
  546.2 43.7 %all-to-all-done.7 = bf16[3,1024,192]{2,0,1:T(4,128)(2,1)} async-done(((bf16[3,1024,192]{2,0,1:T(4,128)(2,1)}), bf16[3,1024,192]{2,0,1:T(4,128)(2,1)}, u32[]{:S(2)}, u32[]{:S(2)}) %all-to-all-start.7) | async-done | bytes 1179680 | tf_op jit(solution)/shard_map/all_to_all | solution.py:207
  589.8 4.6 all-to-all-start.5
  594.6 10.9 convolution_bitcast_fusion
  605.5 11.0 multiply_convert_fusion.1
  619.0 23.2 %all-to-all-done.5 = bf16[3,1024,192]{2,0,1:T(4,128)(2,1)} async-done(((bf16[3,1024,192]{2,0,1:T(4,128)(2,1)}), bf16[3,1024,192]{2,0,1:T(4,128)(2,1)}, u32[]{:S(2)}, u32[]{:S(2)}) %all-to-all-start.5) | async-done | bytes 1179680 | tf_op jit(solution)/shard_map/all_to_all | solution.py:205
  642.2 4.5 all-to-all-start.6
  646.8 4.2 fusion.64
  654.4 9.7 copy.130
  664.1 8.5 fusion.84
  672.6 10.7 reshape.502
  683.4 4.9 convert_reduce_fusion.1
  688.3 4.0 reshape.490
  692.3 4.3 convert_reduce_fusion.3
  696.7 4.0 reshape.488
  700.7 4.9 convert_reduce_fusion.2
  705.6 4.4 reshape.489
  710.0 4.2 fusion.81
  717.4 4.1 fusion.82
  724.7 4.1 fusion.83
  732.2 436.6 %all-reduce.10.cloned.1.call-done = (f32[589824]{0:T(1024)}, f32[589824]{0:T(1024)}, f32[589824]{0:T(1024)}, f32[589824]{0:T(1024)}, f32[2359296]{0:T(1024)}, /*index=5*/f32[2359296]{0:T(1024)}) async-done(((f32[589824]{0:T(1024)}, f32[589824]{0:T(1024)}, f32[589824]{0:T(1024)}, f32[589824]{0:T(1024)}, f32[2359296]{0:T(1024)}, /*index=5*/f32[2359296]{0:T(1024)}), (f32[589824]{0:T(1024)}, f32[589824]{0:T(1024)}, ...) | async-done | bytes 28311568
  1180.3 9.4 add_convert_fusion.4
  1199.9 41.9 %all-reduce.6 = (f32[768]{0:T(1024)}, f32[768]{0:T(1024)}, f32[768]{0:T(1024)}, f32[768]{0:T(1024)}, f32[768]{0:T(1024)}, /*index=5*/f32[768]{0:T(1024)}, f32[76...) all-reduce(f32[768]{0:T(1024)S(1)} %get-tuple-element.328, ...), channel_id=1, replica_groups=mesh['dp'=8,'seq'=4] {'dp','seq'}, use_global_device_ids=true, to_apply=%region_20.21 | all-reduce | flops 10054 | bytes 80432 | tf_op jit(solution)/shard_map/psum | solution.py:243
  1242.3 4.2 add_convert_fusion.3
  1249.9 38.9 %all-gather.9.cloned.1.call-done = f32[589824]{0:T(1024)} async-done(((f32[18432]{0:T(1024)}), f32[589824]{0:T(1024)}) %all-gather.9.cloned.1.call-update) | async-done | bytes 2359312 | tf_op jit(solution)/shard_map/all_gather | solution.py:275
  1292.1 55.6 %all-gather.11.cloned.1.call-done = f32[589824]{0:T(1024)} async-done(((f32[18432]{0:T(1024)}), f32[589824]{0:T(1024)}) %all-gather.11.cloned.1.call-update) | async-done | bytes 2359312 | tf_op jit(solution)/shard_map/all_gather | solution.py:276
  1351.1 55.6 %all-gather.13.cloned.1.call-done = f32[589824]{0:T(1024)} async-done(((f32[18432]{0:T(1024)}), f32[589824]{0:T(1024)}) %all-gather.13.cloned.1.call-update) | async-done | bytes 2359312 | tf_op jit(solution)/shard_map/all_gather | solution.py:277
  1410.0 80.8 %all-gather.15.cloned.1.call-done = f32[2359296]{0:T(1024)} async-done(((f32[73728]{0:T(1024)}), f32[2359296]{0:T(1024)}) %all-gather.15.cloned.1.call-update) | async-done | bytes 9437200 | tf_op jit(solution)/shard_map/all_gather | solution.py:278
  1490.8 10.9 reshape.501
  1501.7 72.6 %all-gather.17.cloned.1.call-done = f32[2359296]{0:T(1024)} async-done(((f32[73728]{0:T(1024)}), f32[2359296]{0:T(1024)}) %all-gather.17.cloned.1.call-update) | async-done | bytes 9437200 | tf_op jit(solution)/shard_map/all_gather | solution.py:279
  1574.3 11.3 reshape.503
  (502 shorter events, 277.9 us)
Async XLA Ops:
  7.2 56.4 %copy-start = (bf16[768,768]{1,0:T(8,128)(2,1)S(1)}, bf16[768,768]{1,0:T(8,128)(2,1)}, u32[]{:S(2)}) copy-start(bf16[768,768]{1,0:T(8,128)(2,1)} %param.38) | copy-start | bytes 3538948
  7.2 4.1 copy-start.4
  7.2 4.1 copy-start.53
  7.2 4.1 copy-start.43
  7.2 4.6 copy-start.69
  8.9 4.8 copy-start.49
  13.7 8.5 copy-start.70
  15.9 43.3 %all-to-all-start.1 = ((bf16[3,256,768]{1,0,2:T(4,128)(2,1)}), bf16[3,256,768]{1,0,2:T(4,128)(2,1)S(1)}, u32[]{:S(2)}, u32[]{:S(2)}) async-start(bf16[3,256,768]{1,0,2:T(4,128)(2,1)} %copy.111), calls=%async_computation.1 | async-start | bytes 3145728 | tf_op jit(solution)/shard_map/all_to_all | solution.py:155
  26.0 37.6 %copy-start.71 = (f32[768]{0:T(1024)S(1)}, f32[768]{0:T(1024)}, u32[]{:S(2)}) copy-start(f32[768]{0:T(1024)} %param.39) | copy-start | bytes 9220
  59.2 40.9 %all-to-all-start = ((bf16[3,256,768]{1,0,2:T(4,128)(2,1)}), bf16[3,256,768]{1,0,2:T(4,128)(2,1)}, u32[]{:S(2)}, u32[]{:S(2)}) async-start(bf16[3,256,768]{1,0,2:T(4,128)(2,1)} %copy.108), calls=%async_computation | async-start | bytes 3145728 | tf_op jit(solution)/shard_map/all_to_all | solution.py:154
  66.9 38.0 %copy-start.65 = (s32[3]{0:T(128)S(1)}, s32[3]{0:T(128)}, u32[]{:S(2)}) copy-start(s32[3]{0:T(128)} %param.30) | copy-start | bytes 40
  100.1 41.3 %all-to-all-start.2 = ((bf16[3,256,768]{1,0,2:T(4,128)(2,1)}), bf16[3,256,768]{1,0,2:T(4,128)(2,1)}, u32[]{:S(2)}, u32[]{:S(2)}) async-start(bf16[3,256,768]{1,0,2:T(4,128)(2,1)} %copy.114), calls=%async_computation.2 | async-start | bytes 3145728 | tf_op jit(solution)/shard_map/all_to_all | solution.py:156
  143.0 4.6 copy-start.28
  143.0 4.6 copy-start.29
  197.4 55.5 %copy-start.7 = (bf16[3,1024,3,64]{1,3,2,0:T(8,128)(2,1)}, bf16[3,1024,3,64]{1,3,2,0:T(8,128)(2,1)S(1)}, u32[]{:S(2)}) copy-start(bf16[3,1024,3,64]{1,3,2,0:T(8,128)(2,1)S(1)} %get-tuple-element.910) | copy-start | bytes 3538948
  197.4 55.5 %copy-start.30 = (pred[3,1024]{1,0:T(4,128)(4,1)}, pred[3,1024]{1,0:T(4,128)(4,1)S(1)}, u32[]{:S(2)}) copy-start(pred[3,1024]{1,0:T(4,128)(4,1)S(1)} %get-tuple-element.943) | copy-start | bytes 9220
  252.9 5.8 copy-start.5
  252.9 5.8 copy-start.72
  261.6 40.2 %copy-start.8 = (f32[768,768]{1,0:T(8,128)}, f32[768,768]{1,0:T(8,128)S(1)}, u32[]{:S(2)}) copy-start(f32[768,768]{1,0:T(8,128)S(1)} %get-tuple-element.462) | copy-start | bytes 7077892
  261.7 40.1 %copy-start.35 = (f32[768]{0:T(1024)}, f32[768]{0:T(1024)S(1)}, u32[]{:S(2)}) copy-start(f32[768]{0:T(1024)S(1)} %broadcast_multiply_fusion) | copy-start | bytes 9220
  261.7 7.9 slice-start.2
  262.4 39.4 %copy-start.37 = (f32[768]{0:T(1024)}, f32[768]{0:T(1024)S(1)}, u32[]{:S(2)}) copy-start(f32[768]{0:T(1024)S(1)} %fusion.70) | copy-start | bytes 9220
  262.4 7.1 copy-start.18
  262.4 7.2 copy-start.58
  262.4 7.2 slice-start.3
  262.4 34.5 %slice-start = ((s8[4718592]{0:T(1024)(128)(4,1)}), s8[4194304]{0:T(1024)(128)(4,1)S(1)}, s32[]{:S(2)}) async-start(s8[4718592]{0:T(1024)(128)(4,1)} %bitcast.259), calls=%async_computation.15 | async-start | bytes 8388608
  269.5 27.4 %copy-start.13 = (f32[768,3072]{1,0:T(8,128)}, f32[768,3072]{1,0:T(8,128)S(1)}, u32[]{:S(2)}) copy-start(f32[768,3072]{1,0:T(8,128)S(1)} %fusion.73) | copy-start | bytes 28311556
  269.6 27.3 %slice-start.1 = ((s8[4718592]{0:T(1024)(128)(4,1)}), s8[524288]{0:T(1024)(128)(4,1)S(1)}, s32[]{:S(2)}) async-start(s8[4718592]{0:T(1024)(128)(4,1)} %bitcast.259), calls=%async_computation.16 | async-start | bytes 1048576
  296.9 4.8 copy-start.20
  307.3 40.0 %all-to-all-start.4 = ((bf16[3,256,768]{1,0,2:T(4,128)(2,1)}), bf16[3,256,768]{1,0,2:T(4,128)(2,1)S(1)}, u32[]{:S(2)}, u32[]{:S(2)}) async-start(bf16[3,256,768]{1,0,2:T(4,128)(2,1)} %copy.119), calls=%async_computation.4 | async-start | bytes 3145728 | tf_op jit(solution)/shard_map/all_to_all | solution.py:197
  366.9 3.7 copy-start.2
  390.8 3.7 copy-start.2
  394.5 3.8 copy-start.3
  427.2 3.7 copy-start.2
  451.1 3.7 copy-start.2
  454.8 3.8 copy-start.3
  487.4 3.7 copy-start.2
  515.0 3.8 copy-start.3
  537.5 4.6 copy-start.6
  537.5 4.6 copy-start.44
  537.5 4.6 copy-start.50
  537.5 4.7 copy-start.54
  537.5 4.7 copy-start.55
  537.5 6.2 copy-start.16
  537.5 52.3 %all-to-all-start.7 = ((bf16[3,1024,192]{2,0,1:T(4,128)(2,1)}), bf16[3,1024,192]{2,0,1:T(4,128)(2,1)}, u32[]{:S(2)}, u32[]{:S(2)}) async-start(bf16[3,1024,192]{2,0,1:T(4,128)(2,1)} %copy.126), calls=%async_computation.7 | async-start | bytes 4194304 | tf_op jit(solution)/shard_map/all_to_all | solution.py:207
  546.2 48.4 %copy-start.36 = (f32[768]{0:T(1024)S(1)}, f32[768]{0:T(1024)}, u32[]{:S(2)}) copy-start(f32[768]{0:T(1024)} %copy-done.35) | copy-start | bytes 9220
  546.2 48.4 %copy-start.38 = (f32[768]{0:T(1024)S(1)}, f32[768]{0:T(1024)}, u32[]{:S(2)}) copy-start(f32[768]{0:T(1024)} %copy-done.37) | copy-start | bytes 9220
  546.2 48.4 %copy-start.40 = (f32[768]{0:T(1024)S(1)}, f32[768]{0:T(1024)}, u32[]{:S(2)}) copy-start(f32[768]{0:T(1024)} %param.42) | copy-start | bytes 9220
  546.2 48.4 %copy-start.42 = (f32[768]{0:T(1024)S(1)}, f32[768]{0:T(1024)}, u32[]{:S(2)}) copy-start(f32[768]{0:T(1024)} %param.43) | copy-start | bytes 9220
  589.8 52.4 %all-to-all-start.5 = ((bf16[3,1024,192]{2,0,1:T(4,128)(2,1)}), bf16[3,1024,192]{2,0,1:T(4,128)(2,1)}, u32[]{:S(2)}, u32[]{:S(2)}) async-start(bf16[3,1024,192]{2,0,1:T(4,128)(2,1)} %copy.122), calls=%async_computation.5 | async-start | bytes 4194304 | tf_op jit(solution)/shard_map/all_to_all | solution.py:205
  594.5 10.9 copy-start.59
  605.4 11.0 copy-start.17
  619.0 27.8 %copy-start.25 = (bf16[768,768]{1,0:T(8,128)(2,1)S(1)}, bf16[768,768]{1,0:T(8,128)(2,1)}, u32[]{:S(2)}) copy-start(bf16[768,768]{1,0:T(8,128)(2,1)} %copy-done.24) | copy-start | bytes 3538948
  642.2 58.4 %all-to-all-start.6 = ((bf16[3,1024,192]{2,0,1:T(4,128)(2,1)}), bf16[3,1024,192]{2,0,1:T(4,128)(2,1)}, u32[]{:S(2)}, u32[]{:S(2)}) async-start(bf16[3,1024,192]{2,0,1:T(4,128)(2,1)} %copy.124), calls=%async_computation.6 | async-start | bytes 4194304 | tf_op jit(solution)/shard_map/all_to_all | solution.py:206
  646.7 522.1 %all-reduce.10.cloned.1.call-start = ((), (), s32[]{:S(2)}) async-start(), calls=%async_computation.14 | async-start | bytes 56623104
  654.4 9.7 copy-start.19
  732.1 447.3 %copy-start.63 = (s32[3,256]{1,0:T(4,128)S(1)}, s32[3,256]{1,0:T(4,128)}, u32[]{:S(2)}) copy-start(s32[3,256]{1,0:T(4,128)} %param.31) | copy-start | bytes 9220
  732.1 514.4 %all-gather.7.cloned.1.call-start = ((), (), s32[]{:S(2)}) async-start(), calls=%async_computation.8 | async-start | bytes 2433024 | tf_op jit(solution)/shard_map/all_gather | solution.py:274
  1170.3 118.5 %all-gather.9.cloned.1.call-start = ((), (), s32[]{:S(2)}) async-start(), calls=%async_computation.9 | async-start | bytes 2433024 | tf_op jit(solution)/shard_map/all_gather | solution.py:275
  1171.9 175.8 %all-gather.11.cloned.1.call-start = ((), (), s32[]{:S(2)}) async-start(), calls=%async_computation.10 | async-start | bytes 2433024 | tf_op jit(solution)/shard_map/all_gather | solution.py:276
  1173.5 233.1 %all-gather.13.cloned.1.call-start = ((), (), s32[]{:S(2)}) async-start(), calls=%async_computation.11 | async-start | bytes 2433024 | tf_op jit(solution)/shard_map/all_gather | solution.py:277
  1175.1 315.7 %all-gather.15.cloned.1.call-start = ((), (), s32[]{:S(2)}) async-start(), calls=%async_computation.12 | async-start | bytes 9732096 | tf_op jit(solution)/shard_map/all_gather | solution.py:278
  1176.9 397.4 %all-gather.17.cloned.1.call-start = ((), (), s32[]{:S(2)}) async-start(), calls=%async_computation.13 | async-start | bytes 9732096 | tf_op jit(solution)/shard_map/all_gather | solution.py:279
  1180.3 11.6 copy-start.26
  (70 other events, 145.4 us)
Sparse Core Ops, SparseCore 0:
  732.3 436.4 all-reduce.9
  1172.1 57.0 all-gather.6
  1232.6 56.1 all-gather.8
  1291.5 56.2 all-gather.10
  1350.4 56.2 all-gather.12
  1409.8 80.9 all-gather.14
  1493.6 80.6 all-gather.16
where the time goes:
time: 1600 us; the launch traced here: 1590 us
  waiting for transfers between devices  928 us (58%)
  local copies, waits for them, and re-layouts  257 us (16%)
  matrix products  188 us (12%)
  blocking collectives  93.2 us (6%)
  other arithmetic  77.4 us (5%)
  starting transfers between devices  33.4 us (2%)
    unnamed x8, waiting for transfers between devices  437 us
    all_gather x1, waiting for transfers between devices, on_device(): lax.all_gather(part_up, ('dp', 'seq'), axis=0, tiled=True)  80.8 us
    all_gather x1, waiting for transfers between devices, on_device(): lax.all_gather(part_down, ('dp', 'seq'), axis=0, tiled=True)  72.6 us
    all_gather x1, waiting for transfers between devices, on_device(): lax.all_gather(part_value, ('dp', 'seq'), axis=0, tiled=True)  55.6 us
    all_gather x1, waiting for transfers between devices, on_device(): lax.all_gather(part_out, ('dp', 'seq'), axis=0, tiled=True)  55.6 us
    all_to_all x1, blocking collectives, on_device(): lax.all_to_all(mixed, 'seq', split_axis=1, concat_axis=2, tiled=True)  51.3 us
    dynamic_update_slice x12, local copies, waits for them, and re-layouts, attend_backward(): lax.scan(visit, (start, start), (query_blocks, grad_blocks, logsum))  50.6 us
    all_to_all x1, waiting for transfers between devices, on_device(): lax.all_to_all(grad_value, 'seq', split_axis=1, concat_axis=2, tiled=True)  43.7 us
  transfers between devices with their start and end apart: 14, of which 12 were waited for; matrix products, arithmetic and copies ran while one was open for 10% of the time, Pallas kernels for 0%

commit v1 on v0

--- a/solution.py
+++ b/solution.py
@@ -2,6 +2,7 @@
 import jax.numpy as jnp
 from jax import lax
 from jax.sharding import PartitionSpec as P
+from jax.lax import all_to_all, axis_size
 
 HEAD = 64
 CLASSES = 70
@@ -150,10 +151,13 @@
     query = (matmul(normed, w_query) + b_query).astype(jnp.bfloat16).reshape(seqs, span, width)
     key = (matmul(normed, w_key) + b_key).astype(jnp.bfloat16).reshape(seqs, span, width)
     value = (matmul(normed, w_value) + b_value).astype(jnp.bfloat16).reshape(seqs, span, width)
+    obtain_cells = lambda x0: jnp.concatenate(
+        all_to_all(jnp.stack(jnp.split(x0, axis_size("seq"), 2)), "seq", 0, 0), 1
+    )
     head_query, head_key, head_value = (
         lax.all_to_all(query, "seq", split_axis=2, concat_axis=1, tiled=True),
         lax.all_to_all(key, "seq", split_axis=2, concat_axis=1, tiled=True),
-        lax.all_to_all(value, "seq", split_axis=2, concat_axis=1, tiled=True),
+        obtain_cells(value),
     )
     count = head_query.shape[1]
     heads = head_query.shape[2] // HEAD

time: 1600 us -> 1600 us (level)
  transfers between devices with their start and end apart: 14 -> 14, of which waited for: 12 -> 12; matrix products, arithmetic and copies ran while one was open for 10% -> 11% of each run, Pallas kernels for 0% -> 0%
where the time goes in v1:
time: 1600 us; the launch traced here: 1580 us
  waiting for transfers between devices  915 us (57%)
  local copies, waits for them, and re-layouts  259 us (16%)
  matrix products  187 us (12%)
  blocking collectives  93.2 us (6%)
  other arithmetic  79.8 us (5%)
  starting transfers between devices  33.4 us (2%)
    unnamed x8, waiting for transfers between devices  437 us
    all_gather x1, waiting for transfers between devices, on_device(): lax.all_gather(part_up, ('dp', 'seq'), axis=0, tiled=True)  80.8 us
    all_gather x1, waiting for transfers between devices, on_device(): lax.all_gather(part_down, ('dp', 'seq'), axis=0, tiled=True)  72.6 us
    all_gather x1, waiting for transfers between devices, on_device(): lax.all_gather(part_value, ('dp', 'seq'), axis=0, tiled=True)  55.6 us
    all_gather x1, waiting for transfers between devices, on_device(): lax.all_gather(part_out, ('dp', 'seq'), axis=0, tiled=True)  55.6 us
    all_to_all x1, blocking collectives, on_device(): lax.all_to_all(mixed, 'seq', split_axis=1, concat_axis=2, tiled=True)  51.3 us
    dynamic_update_slice x12, local copies, waits for them, and re-layouts, attend_backward(): lax.scan(visit, (start, start), (query_blocks, grad_blocks, logsum))  50.7 us
    all_to_all x1, waiting for transfers between devices, on_device(): lax.all_to_all(grad_value, 'seq', split_axis=1, concat_axis=2, tiled=True)  43.7 us
  transfers between devices with their start and end apart: 14, of which 12 were waited for; matrix products, arithmetic and copies ran while one was open for 11% of the time, Pallas kernels for 0%

profile of v1, /device:TPU:0, one launch (start us, length us, event | category | flops | bytes accessed | tf_op | source)
XLA Modules:
  0.0 1584.2 jit_solution(11303392459551659057)
XLA Ops:
  15.9 6.3 all-to-all-start.1
  22.2 3.7 add_convert_fusion.8
  26.0 3.6 copy.135
  29.5 29.6 %all-to-all-done.1 = bf16[3,256,768]{1,0,2:T(4,128)(2,1)S(1)} async-done(((bf16[3,256,768]{1,0,2:T(4,128)(2,1)}), bf16[3,256,768]{1,0,2:T(4,128)(2,1)S(1)}, u32[]{:S(2)}, u32[]{:S(2)}) %all-to-all-start.1) | async-done | bytes 1179680 | tf_op jit(solution)/shard_map/all_to_all | solution.py:159
  59.2 4.4 all-to-all-start
  74.3 25.8 %all-to-all-done = bf16[3,256,768]{1,0,2:T(4,128)(2,1)} async-done(((bf16[3,256,768]{1,0,2:T(4,128)(2,1)}), bf16[3,256,768]{1,0,2:T(4,128)(2,1)}, u32[]{:S(2)}, u32[]{:S(2)}) %all-to-all-start) | async-done | bytes 1179680 | tf_op jit(solution)/shard_map/all_to_all | solution.py:158
  100.1 4.7 all-to-all-start.2
  116.0 16.9 %all-to-all-done.2 = bf16[4,3,256,192]{2,3,1,0:T(8,128)(2,1)} async-done(((bf16[4,3,256,192]{2,3,1,0:T(8,128)(2,1)}), bf16[4,3,256,192]{2,3,1,0:T(8,128)(2,1)}, u32[]{:S(2)}, u32[]{:S(2)}) %all-to-all-start.2) | async-done | bytes 1179680 | tf_op jit(solution)/shard_map/all_to_all | solution.py:155
  144.8 43.8 %while.54 = (s32[]{:T(128)}, bf16[3,1024,192]{1,2,0:T(8,128)(2,1)}, f32[3,2,3,512]{3,2,1,0:T(4,128)}, bf16[3,1024,3,64]{1,3,2,0:T(8,128)(2,1)}, bf16[3,1024,3,64...) while((s32[]{:T(128)}, bf16[3,1024,192]{1,2,0:T(8,128)(2,1)}, ...), condition=%wide.region_7.8_spmd, body=%wide.region_2.7_spmd.sunk | while | flops 420051456 | bytes 28114308 | solution.py:170
  148.2 8.6 while.57
  162.7 8.6 while.57
  177.2 8.6 while.57
  188.6 4.3 copy.146
  192.9 51.3 %all_to_all.98 = bf16[3,1024,192]{2,0,1:T(4,128)(2,1)S(1)} all-to-all(bf16[3,1024,192]{2,0,1:T(4,128)(2,1)} %copy.146), channel_id=1, replica_groups=mesh['dp'=8,'seq'=4] {'seq'}, dimensions={1} | all-to-all | bytes 2359296 | tf_op jit(solution)/shard_map/all_to_all | solution.py:174
  253.7 7.1 fusion.73
  260.8 27.3 %convert_reduce_fusion = (f32[3072]{0:T(1024)}, bf16[768,3072]{1,0:T(8,128)(2,1)S(1)}, f32[768,3072]{1,0:T(8,128)}) fusion(f32[768,3072]{1,0:T(8,128)S(1)} %fusion.73, f32[3072]{0:T(1024)S(1)} %copy-done.58, bf16[768,768]{1,0:T(8,128)(2,1)S(1)} %bitcast.249, bf16[3072,768]{1,0:T(8,128)(2,1)S(1)} %bitcast.267), kind=kOutput, calls=%fused_computation.74 | convolution fusion | flops 3800822784 | bytes 29515776 | tf_op jit(solution)/shard_map/dot_general | solution.py:23
  288.2 4.8 multiply_reduce_fusion.1
  298.6 4.0 all-to-all-start.4
  302.5 36.0 %all-to-all-done.4 = bf16[3,256,768]{1,0,2:T(4,128)(2,1)S(1)} async-done(((bf16[3,256,768]{1,0,2:T(4,128)(2,1)}), bf16[3,256,768]{1,0,2:T(4,128)(2,1)S(1)}, u32[]{:S(2)}, u32[]{:S(2)}) %all-to-all-start.4) | async-done | bytes 1179680 | tf_op jit(solution)/shard_map/all_to_all | solution.py:201
  344.0 181.1 %while.56 = (s32[]{:T(128)}, bf16[3,1024,192]{1,2,0:T(8,128)(2,1)}, bf16[3,1024,192]{1,2,0:T(8,128)(2,1)}, bf16[3,1024,192]{1,2,0:T(8,128)(2,1)}, bf16[3,1024,3,...) while((s32[]{:T(128)}, bf16[3,1024,192]{1,2,0:T(8,128)(2,1)}, ...), condition=%wide.region_16.17_spmd, body=%wide.region_12.16_spmd.sunk | while | flops 1034713664 | bytes 145711024 | solution.py:204
  351.0 48.2 %while.58 = (s32[]{:T(128)}, f32[1024,3,64]{0,2,1:T(8,128)S(1)}, f32[1024,3,64]{0,2,1:T(8,128)}, f32[2,512,3,64]{1,0,3,2:T(2,128)}, bf16[2,512,3,64]{1,3,2,0:T(8...) while((s32[]{:T(128)}, f32[1024,3,64]{0,2,1:T(8,128)S(1)}, ...), condition=%wide.region_15.15_spmd.clone, body=%wide.region_13.14_spmd.clone.sunk | while | flops 1031305728 | bytes 117228824 | solution.py:110
  366.9 8.0 dynamic_update_slice.50
  385.9 3.8 fusion.155
  391.2 8.0 dynamic_update_slice.50
  411.4 48.2 %while.58 = (s32[]{:T(128)}, f32[1024,3,64]{0,2,1:T(8,128)S(1)}, f32[1024,3,64]{0,2,1:T(8,128)}, f32[2,512,3,64]{1,0,3,2:T(2,128)}, bf16[2,512,3,64]{1,3,2,0:T(8...) while((s32[]{:T(128)}, f32[1024,3,64]{0,2,1:T(8,128)S(1)}, ...), condition=%wide.region_15.15_spmd.clone, body=%wide.region_13.14_spmd.clone.sunk | while | flops 1031305728 | bytes 117228824 | solution.py:110
  427.3 8.0 dynamic_update_slice.50
  446.3 3.8 fusion.155
  451.5 8.0 dynamic_update_slice.50
  471.8 48.2 %while.58 = (s32[]{:T(128)}, f32[1024,3,64]{0,2,1:T(8,128)S(1)}, f32[1024,3,64]{0,2,1:T(8,128)}, f32[2,512,3,64]{1,0,3,2:T(2,128)}, bf16[2,512,3,64]{1,3,2,0:T(8...) while((s32[]{:T(128)}, f32[1024,3,64]{0,2,1:T(8,128)S(1)}, ...), condition=%wide.region_15.15_spmd.clone, body=%wide.region_13.14_spmd.clone.sunk | while | flops 1031305728 | bytes 117228824 | solution.py:110
  487.7 8.0 dynamic_update_slice.50
  506.6 3.8 fusion.155
  511.9 8.0 dynamic_update_slice.50
  525.1 4.0 copy.155
  529.2 4.6 all-to-all-start.7
  537.8 43.7 %all-to-all-done.7 = bf16[3,1024,192]{2,0,1:T(4,128)(2,1)} async-done(((bf16[3,1024,192]{2,0,1:T(4,128)(2,1)}), bf16[3,1024,192]{2,0,1:T(4,128)(2,1)}, u32[]{:S(2)}, u32[]{:S(2)}) %all-to-all-start.7) | async-done | bytes 1179680 | tf_op jit(solution)/shard_map/all_to_all | solution.py:211
  581.5 4.6 all-to-all-start.5
  586.2 10.9 convolution_bitcast_fusion
  597.1 11.0 multiply_convert_fusion.1
  610.7 23.2 %all-to-all-done.5 = bf16[3,1024,192]{2,0,1:T(4,128)(2,1)} async-done(((bf16[3,1024,192]{2,0,1:T(4,128)(2,1)}), bf16[3,1024,192]{2,0,1:T(4,128)(2,1)}, u32[]{:S(2)}, u32[]{:S(2)}) %all-to-all-start.5) | async-done | bytes 1179680 | tf_op jit(solution)/shard_map/all_to_all | solution.py:209
  633.9 4.5 all-to-all-start.6
  638.4 4.2 fusion.64
  646.0 9.7 copy.163
  655.7 8.5 fusion.85
  664.3 10.7 reshape.501
  675.0 4.9 convert_reduce_fusion.1
  679.9 4.0 reshape.489
  684.0 4.3 convert_reduce_fusion.3
  688.3 4.0 reshape.487
  692.3 4.9 convert_reduce_fusion.2
  697.3 4.4 reshape.488
  701.6 4.1 fusion.82
  709.0 4.1 fusion.83
  716.4 4.1 fusion.84
  723.8 436.6 %all-reduce.10.cloned.1.call-done = (f32[589824]{0:T(1024)}, f32[589824]{0:T(1024)}, f32[589824]{0:T(1024)}, f32[589824]{0:T(1024)}, f32[2359296]{0:T(1024)}, /*index=5*/f32[2359296]{0:T(1024)}) async-done(((f32[589824]{0:T(1024)}, f32[589824]{0:T(1024)}, f32[589824]{0:T(1024)}, f32[589824]{0:T(1024)}, f32[2359296]{0:T(1024)}, /*index=5*/f32[2359296]{0:T(1024)}), (f32[589824]{0:T(1024)}, f32[589824]{0:T(1024)}, ...) | async-done | bytes 28311568
  1172.0 9.4 add_convert_fusion.4
  1191.6 41.9 %all-reduce.6 = (f32[768]{0:T(1024)}, f32[768]{0:T(1024)}, f32[768]{0:T(1024)}, f32[768]{0:T(1024)}, f32[768]{0:T(1024)}, /*index=5*/f32[768]{0:T(1024)}, f32[76...) all-reduce(f32[768]{0:T(1024)S(1)} %get-tuple-element.345, ...), channel_id=1, replica_groups=mesh['dp'=8,'seq'=4] {'dp','seq'}, use_global_device_ids=true, to_apply=%region_20.21 | all-reduce | flops 10054 | bytes 80432 | tf_op jit(solution)/shard_map/psum | solution.py:247
  1234.0 4.2 add_convert_fusion.3
  1241.6 38.9 %all-gather.9.cloned.1.call-done = f32[589824]{0:T(1024)} async-done(((f32[18432]{0:T(1024)}), f32[589824]{0:T(1024)}) %all-gather.9.cloned.1.call-update) | async-done | bytes 2359312 | tf_op jit(solution)/shard_map/all_gather | solution.py:279
  1283.8 55.6 %all-gather.11.cloned.1.call-done = f32[589824]{0:T(1024)} async-done(((f32[18432]{0:T(1024)}), f32[589824]{0:T(1024)}) %all-gather.11.cloned.1.call-update) | async-done | bytes 2359312 | tf_op jit(solution)/shard_map/all_gather | solution.py:280
  1342.7 55.6 %all-gather.13.cloned.1.call-done = f32[589824]{0:T(1024)} async-done(((f32[18432]{0:T(1024)}), f32[589824]{0:T(1024)}) %all-gather.13.cloned.1.call-update) | async-done | bytes 2359312 | tf_op jit(solution)/shard_map/all_gather | solution.py:281
  1401.6 80.8 %all-gather.15.cloned.1.call-done = f32[2359296]{0:T(1024)} async-done(((f32[73728]{0:T(1024)}), f32[2359296]{0:T(1024)}) %all-gather.15.cloned.1.call-update) | async-done | bytes 9437200 | tf_op jit(solution)/shard_map/all_gather | solution.py:282
  1482.5 10.9 reshape.500
  1493.4 72.6 %all-gather.17.cloned.1.call-done = f32[2359296]{0:T(1024)} async-done(((f32[73728]{0:T(1024)}), f32[2359296]{0:T(1024)}) %all-gather.17.cloned.1.call-update) | async-done | bytes 9437200 | tf_op jit(solution)/shard_map/all_gather | solution.py:283
  1565.9 11.3 reshape.502
  (506 shorter events, 281.7 us)
Async XLA Ops:
  7.2 56.4 %copy-start = (bf16[768,768]{1,0:T(8,128)(2,1)S(1)}, bf16[768,768]{1,0:T(8,128)(2,1)}, u32[]{:S(2)}) copy-start(bf16[768,768]{1,0:T(8,128)(2,1)} %param.38) | copy-start | bytes 3538948
  7.2 4.1 copy-start.4
  7.2 4.1 copy-start.53
  7.2 4.1 copy-start.43
  7.2 4.6 copy-start.69
  8.9 4.8 copy-start.49
  13.7 8.5 copy-start.70
  15.9 43.3 %all-to-all-start.1 = ((bf16[3,256,768]{1,0,2:T(4,128)(2,1)}), bf16[3,256,768]{1,0,2:T(4,128)(2,1)S(1)}, u32[]{:S(2)}, u32[]{:S(2)}) async-start(bf16[3,256,768]{1,0,2:T(4,128)(2,1)} %copy.138), calls=%async_computation.1 | async-start | bytes 3145728 | tf_op jit(solution)/shard_map/all_to_all | solution.py:159
  26.0 37.6 %copy-start.71 = (f32[768]{0:T(1024)S(1)}, f32[768]{0:T(1024)}, u32[]{:S(2)}) copy-start(f32[768]{0:T(1024)} %param.39) | copy-start | bytes 9220
  59.2 40.9 %all-to-all-start = ((bf16[3,256,768]{1,0,2:T(4,128)(2,1)}), bf16[3,256,768]{1,0,2:T(4,128)(2,1)}, u32[]{:S(2)}, u32[]{:S(2)}) async-start(bf16[3,256,768]{1,0,2:T(4,128)(2,1)} %copy.135), calls=%async_computation | async-start | bytes 3145728 | tf_op jit(solution)/shard_map/all_to_all | solution.py:158
  72.0 32.9 %copy-start.65 = (s32[3]{0:T(128)S(1)}, s32[3]{0:T(128)}, u32[]{:S(2)}) copy-start(s32[3]{0:T(128)} %param.30) | copy-start | bytes 40
  100.1 32.8 %all-to-all-start.2 = ((bf16[4,3,256,192]{2,3,1,0:T(8,128)(2,1)}), bf16[4,3,256,192]{2,3,1,0:T(8,128)(2,1)}, u32[]{:S(2)}, u32[]{:S(2)}) async-start(bf16[4,3,256,192]{2,3,1,0:T(8,128)(2,1)} %pad_maximum_fusion.4), calls=%async_computation.2 | async-start | bytes 2359296 | tf_op jit(solution)/shard_map/all_to_all | solution.py:155
  132.9 5.9 copy-start.28
  132.9 5.9 copy-start.29
  188.6 55.5 %copy-start.7 = (bf16[3,1024,3,64]{1,3,2,0:T(8,128)(2,1)}, bf16[3,1024,3,64]{1,3,2,0:T(8,128)(2,1)S(1)}, u32[]{:S(2)}) copy-start(bf16[3,1024,3,64]{1,3,2,0:T(8,128)(2,1)S(1)} %get-tuple-element.931) | copy-start | bytes 3538948
  188.6 55.5 %copy-start.30 = (pred[3,1024]{1,0:T(4,128)(4,1)}, pred[3,1024]{1,0:T(4,128)(4,1)S(1)}, u32[]{:S(2)}) copy-start(pred[3,1024]{1,0:T(4,128)(4,1)S(1)} %get-tuple-element.964) | copy-start | bytes 9220
  244.1 5.8 copy-start.5
  244.1 5.8 copy-start.72
  252.8 40.2 %copy-start.8 = (f32[768,768]{1,0:T(8,128)}, f32[768,768]{1,0:T(8,128)S(1)}, u32[]{:S(2)}) copy-start(f32[768,768]{1,0:T(8,128)S(1)} %get-tuple-element.483) | copy-start | bytes 7077892
  252.9 40.1 %copy-start.35 = (f32[768]{0:T(1024)}, f32[768]{0:T(1024)S(1)}, u32[]{:S(2)}) copy-start(f32[768]{0:T(1024)S(1)} %broadcast_multiply_fusion) | copy-start | bytes 9220
  252.9 7.9 slice-start.2
  253.6 39.4 %copy-start.37 = (f32[768]{0:T(1024)}, f32[768]{0:T(1024)S(1)}, u32[]{:S(2)}) copy-start(f32[768]{0:T(1024)S(1)} %fusion.70) | copy-start | bytes 9220
  253.6 7.2 copy-start.18
  253.6 7.2 copy-start.58
  253.6 7.2 slice-start.3
  253.6 34.5 %slice-start = ((s8[4718592]{0:T(1024)(128)(4,1)}), s8[4194304]{0:T(1024)(128)(4,1)S(1)}, s32[]{:S(2)}) async-start(s8[4718592]{0:T(1024)(128)(4,1)} %bitcast.264), calls=%async_computation.15 | async-start | bytes 8388608
  260.8 27.4 %copy-start.13 = (f32[768,3072]{1,0:T(8,128)}, f32[768,3072]{1,0:T(8,128)S(1)}, u32[]{:S(2)}) copy-start(f32[768,3072]{1,0:T(8,128)S(1)} %fusion.73) | copy-start | bytes 28311556
  260.8 27.3 %slice-start.1 = ((s8[4718592]{0:T(1024)(128)(4,1)}), s8[524288]{0:T(1024)(128)(4,1)S(1)}, s32[]{:S(2)}) async-start(s8[4718592]{0:T(1024)(128)(4,1)} %bitcast.264), calls=%async_computation.16 | async-start | bytes 1048576
  288.1 4.8 copy-start.20
  298.6 40.0 %all-to-all-start.4 = ((bf16[3,256,768]{1,0,2:T(4,128)(2,1)}), bf16[3,256,768]{1,0,2:T(4,128)(2,1)S(1)}, u32[]{:S(2)}, u32[]{:S(2)}) async-start(bf16[3,256,768]{1,0,2:T(4,128)(2,1)} %copy.148), calls=%async_computation.4 | async-start | bytes 3145728 | tf_op jit(solution)/shard_map/all_to_all | solution.py:201
  358.2 3.7 copy-start.2
  382.2 3.7 copy-start.2
  385.9 3.8 copy-start.3
  418.6 3.7 copy-start.2
  442.5 3.7 copy-start.2
  446.3 3.8 copy-start.3
  479.0 3.7 copy-start.2
  506.6 3.8 copy-start.3
  529.1 4.6 copy-start.6
  529.1 4.7 copy-start.44
  529.1 4.7 copy-start.50
  529.1 4.7 copy-start.54
  529.1 4.7 copy-start.55
  529.1 6.2 copy-start.16
  529.2 52.4 %all-to-all-start.7 = ((bf16[3,1024,192]{2,0,1:T(4,128)(2,1)}), bf16[3,1024,192]{2,0,1:T(4,128)(2,1)}, u32[]{:S(2)}, u32[]{:S(2)}) async-start(bf16[3,1024,192]{2,0,1:T(4,128)(2,1)} %copy.155), calls=%async_computation.7 | async-start | bytes 4194304 | tf_op jit(solution)/shard_map/all_to_all | solution.py:211
  537.8 48.3 %copy-start.36 = (f32[768]{0:T(1024)S(1)}, f32[768]{0:T(1024)}, u32[]{:S(2)}) copy-start(f32[768]{0:T(1024)} %copy-done.35) | copy-start | bytes 9220
  537.8 48.3 %copy-start.38 = (f32[768]{0:T(1024)S(1)}, f32[768]{0:T(1024)}, u32[]{:S(2)}) copy-start(f32[768]{0:T(1024)} %copy-done.37) | copy-start | bytes 9220
  537.8 48.4 %copy-start.40 = (f32[768]{0:T(1024)S(1)}, f32[768]{0:T(1024)}, u32[]{:S(2)}) copy-start(f32[768]{0:T(1024)} %param.42) | copy-start | bytes 9220
  537.8 48.4 %copy-start.42 = (f32[768]{0:T(1024)S(1)}, f32[768]{0:T(1024)}, u32[]{:S(2)}) copy-start(f32[768]{0:T(1024)} %param.43) | copy-start | bytes 9220
  581.5 52.4 %all-to-all-start.5 = ((bf16[3,1024,192]{2,0,1:T(4,128)(2,1)}), bf16[3,1024,192]{2,0,1:T(4,128)(2,1)}, u32[]{:S(2)}, u32[]{:S(2)}) async-start(bf16[3,1024,192]{2,0,1:T(4,128)(2,1)} %copy.151), calls=%async_computation.5 | async-start | bytes 4194304 | tf_op jit(solution)/shard_map/all_to_all | solution.py:209
  586.2 10.9 copy-start.59
  597.1 11.0 copy-start.17
  610.7 27.7 %copy-start.25 = (bf16[768,768]{1,0:T(8,128)(2,1)S(1)}, bf16[768,768]{1,0:T(8,128)(2,1)}, u32[]{:S(2)}) copy-start(bf16[768,768]{1,0:T(8,128)(2,1)} %copy-done.24) | copy-start | bytes 3538948
  633.9 58.4 %all-to-all-start.6 = ((bf16[3,1024,192]{2,0,1:T(4,128)(2,1)}), bf16[3,1024,192]{2,0,1:T(4,128)(2,1)}, u32[]{:S(2)}, u32[]{:S(2)}) async-start(bf16[3,1024,192]{2,0,1:T(4,128)(2,1)} %copy.153), calls=%async_computation.6 | async-start | bytes 4194304 | tf_op jit(solution)/shard_map/all_to_all | solution.py:210
  638.4 522.1 %all-reduce.10.cloned.1.call-start = ((), (), s32[]{:S(2)}) async-start(), calls=%async_computation.14 | async-start | bytes 56623104
  646.0 9.7 copy-start.19
  723.8 447.3 %copy-start.63 = (s32[3,256]{1,0:T(4,128)S(1)}, s32[3,256]{1,0:T(4,128)}, u32[]{:S(2)}) copy-start(s32[3,256]{1,0:T(4,128)} %param.31) | copy-start | bytes 9220
  723.8 514.4 %all-gather.7.cloned.1.call-start = ((), (), s32[]{:S(2)}) async-start(), calls=%async_computation.8 | async-start | bytes 2433024 | tf_op jit(solution)/shard_map/all_gather | solution.py:278
  1162.0 118.5 %all-gather.9.cloned.1.call-start = ((), (), s32[]{:S(2)}) async-start(), calls=%async_computation.9 | async-start | bytes 2433024 | tf_op jit(solution)/shard_map/all_gather | solution.py:279
  1163.6 175.8 %all-gather.11.cloned.1.call-start = ((), (), s32[]{:S(2)}) async-start(), calls=%async_computation.10 | async-start | bytes 2433024 | tf_op jit(solution)/shard_map/all_gather | solution.py:280
  1165.2 233.1 %all-gather.13.cloned.1.call-start = ((), (), s32[]{:S(2)}) async-start(), calls=%async_computation.11 | async-start | bytes 2433024 | tf_op jit(solution)/shard_map/all_gather | solution.py:281
  1166.8 315.7 %all-gather.15.cloned.1.call-start = ((), (), s32[]{:S(2)}) async-start(), calls=%async_computation.12 | async-start | bytes 9732096 | tf_op jit(solution)/shard_map/all_gather | solution.py:282
  1168.6 397.4 %all-gather.17.cloned.1.call-start = ((), (), s32[]{:S(2)}) async-start(), calls=%async_computation.13 | async-start | bytes 9732096 | tf_op jit(solution)/shard_map/all_gather | solution.py:283
  1172.0 11.6 copy-start.26
  (70 other events, 145.5 us)
Sparse Core Ops, SparseCore 0:
  723.9 436.5 all-reduce.9
  1163.8 57.0 all-gather.6
  1224.2 56.1 all-gather.8
  1283.1 56.2 all-gather.10
  1342.0 56.2 all-gather.12
  1401.5 80.9 all-gather.14
  1485.3 80.6 all-gather.16
